TPU v7x, 32 devices: a whole 2x2x4 slice. The times are simulated.
32 devices in a mesh: groups: 2 (over y), chan: 4 (over z), space: 4 (over x, core).
Axes of the slice: x: 2, y: 2, z: 4, core: 2. Of those that a mesh axis runs over, the one named last changes fastest.
Arguments:
- volume: bfloat16 [2048, 16, 512], P(('groups', 'chan'), 'space'), parts along dimension 0, may hold values from -6 to 6
- out_grad: bfloat16 [2048, 16, 512], P(('groups', 'chan'), 'space'), parts along dimension 0, may hold values from -6 to 6
- weight_in: bfloat16 [1024, 1024], P('chan'), may hold values from -0.1875 to 0.1875
- weight_out: bfloat16 [1024, 1024], P('chan'), may hold values from -0.1875 to 0.1875
- filter_taps: float32 [1024, 27], P('chan'), may hold values from -1.25 to 1.25
- filter_bias: float32 [1024], P('chan'), may hold values from -3 to 3
Outputs:
- block_out: bfloat16 [2048, 16, 512], P(('groups', 'chan'), 'space'), parts along dimension 0
- volume_grad: bfloat16 [2048, 16, 512], P(('groups', 'chan'), 'space'), parts along dimension 0
There are 2 independent parts, one for each index of `groups`. A program takes and returns all parts, laid end to end along the dimension named above; an argument that names none is the same for every part. Nothing has to cross between parts.
All inputs are finite; a program needn't handle non-finite values.
Results may differ from a plain program's by a relative error of at most 0.0085.
Values may be sent and summed in bfloat16 or wider, within the bound.
No kernel may reach another device: no remote copies, remote signals or barrier semaphores. Data moves between devices by JAX's collectives and lax.ppermute only.
A program may use at most 64 MiB of HBM per device.

v0:
```python
import jax
import jax.numpy as jnp
from jax import lax
from jax.sharding import PartitionSpec as P

CX = 32
CY = 16
root_half = 0.7071067811865476
inv_root_two_pi = 0.3989422804014327


def with_halo(block, sides, width):
    for axis, dim in sides:
        count = lax.axis_size(axis)
        forward = [(i, i + 1) for i in range(count - 1)]
        backward = [(target, source) for source, target in forward]
        low = lax.ppermute(
            lax.slice_in_dim(block, block.shape[dim] - width, None, axis=dim), axis, forward
        )
        high = lax.ppermute(lax.slice_in_dim(block, 0, width, axis=dim), axis, backward)
        block = jnp.concatenate([low, block, high], axis=dim)
    return block


def gelu_value(field):
    return 0.5 * field * (1.0 + lax.erf(field * root_half))


def gelu_slope(field):
    return (
        0.5 * (1.0 + lax.erf(field * root_half))
        + field * jnp.exp(-0.5 * field * field) * inv_root_two_pi
    )


def core(padded, filter_taps, direction):
    extent_z = padded.shape[1] - 2
    extent_y = padded.shape[2] - 2
    extent_x = padded.shape[3] - 2
    summed = jnp.zeros((padded.shape[0], extent_z, extent_y, extent_x), jnp.float32)
    for shift_z in range(3):
        for shift_y in range(3):
            for shift_x in range(3):
                tap_index = (shift_z * 3 + shift_y) * 3 + shift_x
                begin_z = 1 + direction * (shift_z - 1)
                begin_y = 1 + direction * (shift_y - 1)
                begin_x = 1 + direction * (shift_x - 1)
                window = padded[
                    :,
                    begin_z : begin_z + extent_z,
                    begin_y : begin_y + extent_y,
                    begin_x : begin_x + extent_x,
                ]
                summed = summed + filter_taps[:, tap_index][:, None, None, None] * window
    return summed


def lift(field_z):
    extended = field_z.astype(jnp.float32).reshape(field_z.shape[0], field_z.shape[1], CY, CX)
    return jnp.pad(extended, ((0, 0), (0, 0), (1, 1), (1, 1)))


def to_cells(field):
    return lax.all_to_all(
        field.reshape(field.shape[0], -1), "chan", split_axis=1, concat_axis=0, tiled=True
    )


def to_channels(field, slab_shape):
    return lax.all_to_all(field, "chan", split_axis=0, concat_axis=1, tiled=True).reshape(
        slab_shape
    )


def body(volume, out_grad, weight_in, weight_out, filter_taps, filter_bias):
    slab_shape = volume.shape
    contract_first = (((0,), (0,)), ((), ()))
    full_in, full_out = (
        lax.all_gather(weight_in, "chan", axis=0, tiled=True),
        lax.all_gather(weight_out, "chan", axis=0, tiled=True),
    )
    vol_cells = to_cells(volume)
    hidden = to_channels(
        jnp.dot(full_in, vol_cells, preferred_element_type=jnp.float32).astype(jnp.bfloat16),
        slab_shape,
    )
    padded = lift(with_halo(hidden, (("space", 1),), 1))
    mixed = core(padded, filter_taps, 1) + filter_bias[:, None, None, None]
    active = gelu_value(mixed).astype(jnp.bfloat16).reshape(slab_shape)
    act_cells = to_cells(active)
    out_cells = vol_cells.astype(jnp.float32) + jnp.dot(
        full_out, act_cells, preferred_element_type=jnp.float32
    )
    block_out = to_channels(out_cells.astype(jnp.bfloat16), slab_shape)
    grad_cells = to_cells(out_grad)
    act_part = lax.dot_general(
        full_out, grad_cells, contract_first, preferred_element_type=jnp.float32
    )
    act_grad = to_channels(act_part.astype(jnp.bfloat16), slab_shape)
    slope = gelu_slope(mixed)
    mix_grad = (
        (act_grad.astype(jnp.float32).reshape(slope.shape) * slope)
        .astype(jnp.bfloat16)
        .reshape(slab_shape)
    )
    padded_grad = lift(with_halo(mix_grad, (("space", 1),), 1))
    hid_grad = core(padded_grad, filter_taps, -1).astype(jnp.bfloat16).reshape(slab_shape)
    hid_cells = to_cells(hid_grad)
    back_part = lax.dot_general(
        full_in, hid_cells, contract_first, preferred_element_type=jnp.float32
    )
    volume_grad = to_channels(
        (grad_cells.astype(jnp.float32) + back_part).astype(jnp.bfloat16), slab_shape
    )
    return (block_out, volume_grad)


def solution(mesh):
    placed = (
        P(("groups", "chan"), "space", None),
        P(("groups", "chan"), "space", None),
        P("chan", None),
        P("chan", None),
        P("chan", None),
        P("chan"),
    )
    return jax.shard_map(
        body,
        mesh=mesh,
        in_specs=placed,
        out_specs=(P(("groups", "chan"), "space", None), P(("groups", "chan"), "space", None)),
        check_vma=False,
    )
```

profile of v0, /device:TPU:0, one launch (start us, length us, event | category | flops | bytes accessed | tf_op | source)
XLA Modules:
  0.0 338.6 jit_solution(1226160043802990815)
XLA Ops:
  7.9 2.5 copy.26
  10.4 6.3 %all-to-all-start = ((bf16[256,4,512]{2,0,1:T(8,128)(2,1)}), bf16[256,4,512]{2,0,1:T(8,128)(2,1)S(1)}, u32[]{:S(2)}, u32[]{:S(2)}) async-start(bf16[256,4,512]{2,0,1:T(8,128)(2,1)} %copy.26), calls=%async_computation | async-start | bytes 2097152 | tf_op jit(solution)/shard_map/all_to_all | solution.py:64
  18.6 49.2 %all-to-all-done = bf16[256,4,512]{2,0,1:T(8,128)(2,1)S(1)} async-done(((bf16[256,4,512]{2,0,1:T(8,128)(2,1)}), bf16[256,4,512]{2,0,1:T(8,128)(2,1)S(1)}, u32[]{:S(2)}, u32[]{:S(2)}) %all-to-all-start) | async-done | bytes 1048608 | tf_op jit(solution)/shard_map/all_to_all | solution.py:64
  67.8 3.5 %all-to-all-start.4 = ((bf16[256,4,512]{2,0,1:T(8,128)(2,1)}), bf16[256,4,512]{2,0,1:T(8,128)(2,1)S(1)}, u32[]{:S(2)}, u32[]{:S(2)}) async-start(bf16[256,4,512]{2,0,1:T(8,128)(2,1)} %copy.31), calls=%async_computation.4 | async-start | bytes 2097152 | tf_op jit(solution)/shard_map/all_to_all | solution.py:64
  71.3 15.1 %all-gather.3.cloned.1.call-done = bf16[1024,1024]{1,0:T(8,128)(2,1)} async-done(((bf16[256,1024]{1,0:T(8,128)(2,1)}), bf16[1024,1024]{1,0:T(8,128)(2,1)}) %all-gather.3.cloned.1.call-update) | async-done | bytes 2097168 | tf_op jit(solution)/shard_map/all_gather | solution.py:79
  86.5 2.8 convolution_convert_fusion.1
  90.7 8.0 %all-to-all-done.4 = bf16[256,4,512]{2,0,1:T(8,128)(2,1)S(1)} async-done(((bf16[256,4,512]{2,0,1:T(8,128)(2,1)}), bf16[256,4,512]{2,0,1:T(8,128)(2,1)S(1)}, u32[]{:S(2)}, u32[]{:S(2)}) %all-to-all-start.4) | async-done | bytes 1048608 | tf_op jit(solution)/shard_map/all_to_all | solution.py:64
  98.7 3.5 %all-to-all-start.1 = ((bf16[4,256,512]{1,2,0:T(8,128)(2,1)}), bf16[4,256,512]{1,2,0:T(8,128)(2,1)S(1)}, u32[]{:S(2)}, u32[]{:S(2)}) async-start(bf16[4,256,512]{1,2,0:T(8,128)(2,1)} %copy.28), calls=%async_computation.1 | async-start | bytes 2097152 | tf_op jit(solution)/shard_map/all_to_all | solution.py:70
  102.3 58.4 %all-gather.5.cloned.1.call-done = bf16[1024,1024]{1,0:T(8,128)(2,1)} async-done(((bf16[256,1024]{1,0:T(8,128)(2,1)}), bf16[1024,1024]{1,0:T(8,128)(2,1)}) %all-gather.5.cloned.1.call-update) | async-done | bytes 2097168 | tf_op jit(solution)/shard_map/all_gather | solution.py:80
  160.6 2.9 convolution_convert_fusion
  164.8 3.6 %all-to-all-start.5 = ((bf16[4,256,512]{1,2,0:T(8,128)(2,1)}), bf16[4,256,512]{1,2,0:T(8,128)(2,1)S(1)}, u32[]{:S(2)}, u32[]{:S(2)}) async-start(bf16[4,256,512]{1,2,0:T(8,128)(2,1)} %copy.33), calls=%async_computation.5 | async-start | bytes 2097152 | tf_op jit(solution)/shard_map/all_to_all | solution.py:70
  172.3 22.0 %all-to-all-done.5 = bf16[4,256,512]{1,2,0:T(8,128)(2,1)S(1)} async-done(((bf16[4,256,512]{1,2,0:T(8,128)(2,1)}), bf16[4,256,512]{1,2,0:T(8,128)(2,1)S(1)}, u32[]{:S(2)}, u32[]{:S(2)}) %all-to-all-start.5) | async-done | bytes 1048608 | tf_op jit(solution)/shard_map/all_to_all | solution.py:70
  195.7 10.0 %fusion.5 = (bf16[256,4,16,32]{0,3,2,1:T(8,128)(2,1)S(1)}, f32[256,4,16,32]{0,3,2,1:T(8,128)S(1)}) fusion(f32[256,4,16,32]{0,3,2,1:T(8,128)S(1)} %bitcast.72, f32[256]{0:T(256)S(1)} %copy-done.5, f32[256]{0:T(256)S(1)} %bitcast.102, f32[256]{0:T(256)S(1)} %bitcast.104, f32[256]{0:T(256)S(1)} %bitcast.108, f32[256]{0:T(256)S(1)} %bitcast.110, ...), kind=kLoop, calls=%fused_computation.54 | loop fusion | flops 33554432 | bytes 14708736 | tf_op jit(solution)/shard_map/convert_element_type | solution.py:103
  210.6 3.5 %all-to-all-start.2 = ((bf16[256,4,512]{0,2,1:T(8,128)(2,1)}), bf16[256,4,512]{0,2,1:T(8,128)(2,1)S(1)}, u32[]{:S(2)}, u32[]{:S(2)}) async-start(bf16[256,4,512]{0,2,1:T(8,128)(2,1)} %bitcast.35), calls=%async_computation.2 | async-start | bytes 2097152 | tf_op jit(solution)/shard_map/all_to_all | solution.py:64
  215.3 10.0 %fusion.104 = bf16[256,4,16,32]{0,3,2,1:T(8,128)(2,1)} fusion(f32[256,6,16,32]{0,3,2,1:T(8,128)S(1)} %maximum_convert_fusion.1, f32[256]{0:T(256)S(1)} %bitcast.103, f32[256]{0:T(256)S(1)} %bitcast.105, f32[256]{0:T(256)S(1)} %bitcast.109, f32[256]{0:T(256)S(1)} %bitcast.111, f32[256]{0:T(256)S(1)} %bitcast.113, f32[256]{0:T(256)S(1)} %bitcast.115, ...), kind=kLoop, calls=%fused_computation.153 | loop fusion | flops 28311552 | bytes 10513408 | tf_op jit(solution)/shard_map/convert_element_type | solution.py:107
  225.4 14.8 %all-to-all-done.2 = bf16[256,4,512]{0,2,1:T(8,128)(2,1)S(1)} async-done(((bf16[256,4,512]{0,2,1:T(8,128)(2,1)}), bf16[256,4,512]{0,2,1:T(8,128)(2,1)S(1)}, u32[]{:S(2)}, u32[]{:S(2)}) %all-to-all-start.2) | async-done | bytes 1048608 | tf_op jit(solution)/shard_map/all_to_all | solution.py:64
  240.2 4.3 %all-to-all-start.6 = ((bf16[256,4,512]{0,2,1:T(8,128)(2,1)}), bf16[256,4,512]{0,2,1:T(8,128)(2,1)}, u32[]{:S(2)}, u32[]{:S(2)}) async-start(bf16[256,4,512]{0,2,1:T(8,128)(2,1)} %bitcast.83), calls=%async_computation.6 | async-start | bytes 2097152 | tf_op jit(solution)/shard_map/all_to_all | solution.py:64
  247.1 3.2 fusion.109
  251.7 19.9 %all-to-all-done.6 = bf16[256,4,512]{0,2,1:T(8,128)(2,1)} async-done(((bf16[256,4,512]{0,2,1:T(8,128)(2,1)}), bf16[256,4,512]{0,2,1:T(8,128)(2,1)}, u32[]{:S(2)}, u32[]{:S(2)}) %all-to-all-start.6) | async-done | bytes 1048608 | tf_op jit(solution)/shard_map/all_to_all | solution.py:64
  271.5 3.7 %all-to-all-start.3 = ((bf16[4,256,512]{2,1,0:T(8,128)(2,1)}), bf16[4,256,512]{2,1,0:T(8,128)(2,1)S(1)}, u32[]{:S(2)}, u32[]{:S(2)}) async-start(bf16[4,256,512]{2,1,0:T(8,128)(2,1)} %bitcast.39), calls=%async_computation.3 | async-start | bytes 2097152 | tf_op jit(solution)/shard_map/all_to_all | solution.py:70
  277.3 3.8 %fusion.108 = bf16[1024,512]{0,1:T(8,128)(2,1)} fusion(bf16[1024,512]{0,1:T(8,128)(2,1)S(1)} %copy.40, bf16[1024,512]{1,0:T(8,128)(2,1)S(1)} %bitcast.85, bf16[1024,1024]{1,0:T(8,128)(2,1)} %all-gather.3.cloned.1.call-done), kind=kOutput, calls=%fused_computation.164 | convolution fusion | flops 1075314688 | bytes 5242880 | tf_op jit(solution)/shard_map/dot_general | solution.py:109
  283.4 17.8 %all-to-all-done.3 = bf16[4,256,512]{2,1,0:T(8,128)(2,1)S(1)} async-done(((bf16[4,256,512]{2,1,0:T(8,128)(2,1)}), bf16[4,256,512]{2,1,0:T(8,128)(2,1)S(1)}, u32[]{:S(2)}, u32[]{:S(2)}) %all-to-all-start.3) | async-done | bytes 1048608 | tf_op jit(solution)/shard_map/all_to_all | solution.py:70
  301.2 3.5 %all-to-all-start.7 = ((bf16[4,256,512]{2,1,0:T(8,128)(2,1)}), bf16[4,256,512]{2,1,0:T(8,128)(2,1)S(1)}, u32[]{:S(2)}, u32[]{:S(2)}) async-start(bf16[4,256,512]{2,1,0:T(8,128)(2,1)} %bitcast.54), calls=%async_computation.7 | async-start | bytes 2097152 | tf_op jit(solution)/shard_map/all_to_all | solution.py:70
  306.5 23.5 %all-to-all-done.7 = bf16[4,256,512]{2,1,0:T(8,128)(2,1)S(1)} async-done(((bf16[4,256,512]{2,1,0:T(8,128)(2,1)}), bf16[4,256,512]{2,1,0:T(8,128)(2,1)S(1)}, u32[]{:S(2)}, u32[]{:S(2)}) %all-to-all-start.7) | async-done | bytes 1048608 | tf_op jit(solution)/shard_map/all_to_all | solution.py:70
  (44 shorter events, 28.3 us)
Async XLA Ops:
  7.2 79.3 %all-gather.3.cloned.1.call-start = ((), (), s32[]{:S(2)}) async-start(), calls=%async_computation.8 | async-start | bytes 2621440 | tf_op jit(solution)/shard_map/all_gather | solution.py:79
  7.9 9.6 %copy-start.2 = (bf16[256,4,512]{2,1,0:T(4,128)(2,1)S(1)}, bf16[256,4,512]{2,1,0:T(4,128)(2,1)}, u32[]{:S(2)}) copy-start(bf16[256,4,512]{2,1,0:T(4,128)(2,1)} %param.7) | copy-start | bytes 3145732
  10.4 57.4 %all-to-all-start = ((bf16[256,4,512]{2,0,1:T(8,128)(2,1)}), bf16[256,4,512]{2,0,1:T(8,128)(2,1)S(1)}, u32[]{:S(2)}, u32[]{:S(2)}) async-start(bf16[256,4,512]{2,0,1:T(8,128)(2,1)} %copy.26), calls=%async_computation | async-start | bytes 2097152 | tf_op jit(solution)/shard_map/all_to_all | solution.py:64
  16.7 143.9 %all-gather.5.cloned.1.call-start = ((), (), s32[]{:S(2)}) async-start(), calls=%async_computation.9 | async-start | bytes 2621440 | tf_op jit(solution)/shard_map/all_gather | solution.py:80
  67.8 21.5 %copy-start = (bf16[256,4,512]{2,0,1:T(8,128)(2,1)}, bf16[256,4,512]{2,0,1:T(8,128)(2,1)S(1)}, u32[]{:S(2)}) copy-start(bf16[256,4,512]{2,0,1:T(8,128)(2,1)S(1)} %all-to-all-done) | copy-start | bytes 3145732
  67.8 30.9 %all-to-all-start.4 = ((bf16[256,4,512]{2,0,1:T(8,128)(2,1)}), bf16[256,4,512]{2,0,1:T(8,128)(2,1)S(1)}, u32[]{:S(2)}, u32[]{:S(2)}) async-start(bf16[256,4,512]{2,0,1:T(8,128)(2,1)} %copy.31), calls=%async_computation.4 | async-start | bytes 2097152 | tf_op jit(solution)/shard_map/all_to_all | solution.py:64
  98.7 66.1 %all-to-all-start.1 = ((bf16[4,256,512]{1,2,0:T(8,128)(2,1)}), bf16[4,256,512]{1,2,0:T(8,128)(2,1)S(1)}, u32[]{:S(2)}, u32[]{:S(2)}) async-start(bf16[4,256,512]{1,2,0:T(8,128)(2,1)} %copy.28), calls=%async_computation.1 | async-start | bytes 2097152 | tf_op jit(solution)/shard_map/all_to_all | solution.py:70
  164.8 7.4 %copy-start.4 = (f32[256,27]{0,1:T(8,128)S(1)}, f32[256,27]{0,1:T(8,128)}, u32[]{:S(2)}) copy-start(f32[256,27]{0,1:T(8,128)} %param.10) | copy-start | bytes 82948
  164.8 29.5 %all-to-all-start.5 = ((bf16[4,256,512]{1,2,0:T(8,128)(2,1)}), bf16[4,256,512]{1,2,0:T(8,128)(2,1)S(1)}, u32[]{:S(2)}, u32[]{:S(2)}) async-start(bf16[4,256,512]{1,2,0:T(8,128)(2,1)} %copy.33), calls=%async_computation.5 | async-start | bytes 2097152 | tf_op jit(solution)/shard_map/all_to_all | solution.py:70
  169.3 25.2 %collective-permute-start = (bf16[256,1,512]{0,2,1:T(8,128)(2,1)}, bf16[256,1,512]{0,2,1:T(8,128)(2,1)S(1)}, u32[]{:S(2)}, u32[]{:S(2)}) collective-permute-start(bf16[256,1,512]{0,2,1:T(8,128)(2,1)} %get-tuple-element.8), channel_id=1, source_target_pairs={{0,1},{1,2},{2,3},{4,5},{5,6},{6,7},{8,9},{9,10},{10,11},{12,13},{... | collective-permute-start | bytes 786440 | tf_op jit(solution)/shard_map/ppermute | solution.py:17
  170.9 23.6 %collective-permute-start.1 = (bf16[256,1,512]{0,2,1:T(8,128)(2,1)}, bf16[256,1,512]{0,2,1:T(8,128)(2,1)}, u32[]{:S(2)}, u32[]{:S(2)}) collective-permute-start(bf16[256,1,512]{0,2,1:T(8,128)(2,1)} %get-tuple-element.9), channel_id=1, source_target_pairs={{1,0},{2,1},{3,2},{5,4},{6,5},{7,6},{9,8},{10,9},{11,10},{13,12},{... | collective-permute-start | bytes 786440 | tf_op jit(solution)/shard_map/ppermute | solution.py:20
  194.5 1.2 copy-start.5
  206.6 7.5 %collective-permute-start.2 = (bf16[256,1,512]{0,2,1:T(8,128)(2,1)}, bf16[256,1,512]{0,2,1:T(8,128)(2,1)S(1)}, u32[]{:S(2)}, u32[]{:S(2)}) collective-permute-start(bf16[256,1,512]{0,2,1:T(8,128)(2,1)} %get-tuple-element.6), channel_id=1, source_target_pairs={{0,1},{1,2},{2,3},{4,5},{5,6},{6,7},{8,9},{9,10},{10,11},{12,13},{... | collective-permute-start | bytes 786440 | tf_op jit(solution)/shard_map/ppermute | solution.py:17
  207.9 6.2 %collective-permute-start.3 = (bf16[256,1,512]{0,2,1:T(8,128)(2,1)}, bf16[256,1,512]{0,2,1:T(8,128)(2,1)}, u32[]{:S(2)}, u32[]{:S(2)}) collective-permute-start(bf16[256,1,512]{0,2,1:T(8,128)(2,1)} %get-tuple-element.7), channel_id=1, source_target_pairs={{1,0},{2,1},{3,2},{5,4},{6,5},{7,6},{9,8},{10,9},{11,10},{13,12},{... | collective-permute-start | bytes 786440 | tf_op jit(solution)/shard_map/ppermute | solution.py:20
  210.6 29.6 %all-to-all-start.2 = ((bf16[256,4,512]{0,2,1:T(8,128)(2,1)}), bf16[256,4,512]{0,2,1:T(8,128)(2,1)S(1)}, u32[]{:S(2)}, u32[]{:S(2)}) async-start(bf16[256,4,512]{0,2,1:T(8,128)(2,1)} %bitcast.35), calls=%async_computation.2 | async-start | bytes 2097152 | tf_op jit(solution)/shard_map/all_to_all | solution.py:64
  225.4 19.1 %copy-start.1 = (bf16[256,4,512]{2,0,1:T(8,128)(2,1)S(1)}, bf16[256,4,512]{2,0,1:T(8,128)(2,1)}, u32[]{:S(2)}) copy-start(bf16[256,4,512]{2,0,1:T(8,128)(2,1)} %copy-done) | copy-start | bytes 3145732
  240.2 31.3 %all-to-all-start.6 = ((bf16[256,4,512]{0,2,1:T(8,128)(2,1)}), bf16[256,4,512]{0,2,1:T(8,128)(2,1)}, u32[]{:S(2)}, u32[]{:S(2)}) async-start(bf16[256,4,512]{0,2,1:T(8,128)(2,1)} %bitcast.83), calls=%async_computation.6 | async-start | bytes 2097152 | tf_op jit(solution)/shard_map/all_to_all | solution.py:64
  245.8 1.3 copy-start.3
  271.5 29.6 %all-to-all-start.3 = ((bf16[4,256,512]{2,1,0:T(8,128)(2,1)}), bf16[4,256,512]{2,1,0:T(8,128)(2,1)S(1)}, u32[]{:S(2)}, u32[]{:S(2)}) async-start(bf16[4,256,512]{2,1,0:T(8,128)(2,1)} %bitcast.39), calls=%async_computation.3 | async-start | bytes 2097152 | tf_op jit(solution)/shard_map/all_to_all | solution.py:70
  301.2 28.8 %all-to-all-start.7 = ((bf16[4,256,512]{2,1,0:T(8,128)(2,1)}), bf16[4,256,512]{2,1,0:T(8,128)(2,1)S(1)}, u32[]{:S(2)}, u32[]{:S(2)}) async-start(bf16[4,256,512]{2,1,0:T(8,128)(2,1)} %bitcast.54), calls=%async_computation.7 | async-start | bytes 2097152 | tf_op jit(solution)/shard_map/all_to_all | solution.py:70
Sparse Core Ops, SparseCore 0:
  9.5 76.9 all-gather.2
  88.1 72.5 all-gather.4
where the time goes:
time: 340 us; the launch traced here: 339 us
  waiting for transfers between devices  230 us (68%)
  starting transfers between devices  37.6 us (11%)
  other arithmetic  24 us (7%)
  local copies, waits for them, and re-layouts  19.9 us (6%)
  between operations  14.3 us (4%)
  matrix products  12.7 us (4%)
    all_to_all x4, waiting for transfers between devices, to_cells(): lax.all_to_all(field.reshape(field.shape[0], -1), 'chan', split_axis=1, c...  91.9 us
    all_to_all x4, waiting for transfers between devices, to_channels(): lax.all_to_all(field, 'chan', split_axis=0, concat_axis=1, tiled=True)  63.2 us
    all_gather x1, waiting for transfers between devices, body(): lax.all_gather(weight_out, 'chan', axis=0, tiled=True)  58.4 us
    all_to_all x4, starting transfers between devices, to_cells(): lax.all_to_all(field.reshape(field.shape[0], -1), 'chan', split_axis=1, c...  17.6 us
    all_gather x1, waiting for transfers between devices, body(): lax.all_gather(weight_in, 'chan', axis=0, tiled=True)  15.1 us
    all_to_all x4, starting transfers between devices, to_channels(): lax.all_to_all(field, 'chan', split_axis=0, concat_axis=1, tiled=True)  14.4 us
    convert_element_type x1, other arithmetic, body(): core(padded_grad, filter_taps, -1).astype(jnp.bfloat16).reshape(slab_shape)  10 us
    convert_element_type x1, other arithmetic, body(): mix_grad = (act_grad.astype(jnp.float32).reshape(slope.shape) * slope).as...  10 us
  transfers between devices with their start and end apart: 14, of which 9 were waited for; matrix products, arithmetic and copies ran while one was open for 13% of the time, Pallas kernels for 0%

commit v1 on v0

--- a/solution.py
+++ b/solution.py
@@ -61,8 +61,14 @@
 
 
 def to_cells(field):
-    return lax.all_to_all(
-        field.reshape(field.shape[0], -1), "chan", split_axis=1, concat_axis=0, tiled=True
+    return jnp.concatenate(
+        lax.all_to_all(
+            jnp.stack(jnp.split(field.reshape(field.shape[0], -1), lax.axis_size("chan"), axis=1)),
+            "chan",
+            0,
+            0,
+        ),
+        axis=0,
     )
 
 

time: 340 us -> 340 us (level)
    another operation x0 -> x4, other arithmetic: none -> 4.45 us  [to_cells(): jnp.stack(jnp.split(field.reshape(field.shape[0], -1), lax.axis_size('cha...]
where the time goes in v1:
time: 340 us; the launch traced here: 339 us
  waiting for transfers between devices  229 us (67%)
  starting transfers between devices  37.5 us (11%)
  other arithmetic  26.8 us (8%)
  local copies, waits for them, and re-layouts  17.8 us (5%)
  between operations  14.4 us (4%)
  matrix products  12.8 us (4%)
    all_to_all x4, waiting for transfers between devices, to_cells(): lax.all_to_all(jnp.stack(jnp.split(field.reshape(field.shape[0], -1), lax...  91.1 us
    all_to_all x4, waiting for transfers between devices, to_channels(): lax.all_to_all(field, 'chan', split_axis=0, concat_axis=1, tiled=True)  63.4 us
    all_gather x1, waiting for transfers between devices, body(): lax.all_gather(weight_out, 'chan', axis=0, tiled=True)  58.3 us
    all_to_all x4, starting transfers between devices, to_cells(): lax.all_to_all(jnp.stack(jnp.split(field.reshape(field.shape[0], -1), lax...  17.8 us
    all_gather x1, waiting for transfers between devices, body(): lax.all_gather(weight_in, 'chan', axis=0, tiled=True)  15.2 us
    all_to_all x4, starting transfers between devices, to_channels(): lax.all_to_all(field, 'chan', split_axis=0, concat_axis=1, tiled=True)  14.2 us
    convert_element_type x1, other arithmetic, body(): mix_grad = (act_grad.astype(jnp.float32).reshape(slope.shape) * slope).as...  10 us
    convert_element_type x1, other arithmetic, body(): core(padded_grad, filter_taps, -1).astype(jnp.bfloat16).reshape(slab_shape)  9.32 us
  transfers between devices with their start and end apart: 14, of which 9 were waited for; matrix products, arithmetic and copies ran while one was open for 13% of the time, Pallas kernels for 0%

profile of v1, /device:TPU:0, one launch (start us, length us, event | category | flops | bytes accessed | tf_op | source)
XLA Modules:
  0.0 338.7 jit_solution(14345214376379707854)
XLA Ops:
  10.6 6.3 %all-to-all-start = ((bf16[4,256,512]{2,1,0:T(8,128)(2,1)}), bf16[4,256,512]{2,1,0:T(8,128)(2,1)S(1)}, u32[]{:S(2)}, u32[]{:S(2)}) async-start(bf16[4,256,512]{2,1,0:T(8,128)(2,1)} %pad_maximum_fusion), calls=%async_computation | async-start | bytes 2097152 | tf_op jit(solution)/shard_map/all_to_all | solution.py:65
  19.2 48.9 %all-to-all-done = bf16[4,256,512]{2,1,0:T(8,128)(2,1)S(1)} async-done(((bf16[4,256,512]{2,1,0:T(8,128)(2,1)}), bf16[4,256,512]{2,1,0:T(8,128)(2,1)S(1)}, u32[]{:S(2)}, u32[]{:S(2)}) %all-to-all-start) | async-done | bytes 1048608 | tf_op jit(solution)/shard_map/all_to_all | solution.py:65
  68.1 3.5 %all-to-all-start.4 = ((bf16[4,256,512]{2,1,0:T(8,128)(2,1)}), bf16[4,256,512]{2,1,0:T(8,128)(2,1)S(1)}, u32[]{:S(2)}, u32[]{:S(2)}) async-start(bf16[4,256,512]{2,1,0:T(8,128)(2,1)} %pad_maximum_fusion.2), calls=%async_computation.4 | async-start | bytes 2097152 | tf_op jit(solution)/shard_map/all_to_all | solution.py:65
  71.6 15.2 %all-gather.3.cloned.1.call-done = bf16[1024,1024]{1,0:T(8,128)(2,1)} async-done(((bf16[256,1024]{1,0:T(8,128)(2,1)}), bf16[1024,1024]{1,0:T(8,128)(2,1)}) %all-gather.3.cloned.1.call-update) | async-done | bytes 2097168 | tf_op jit(solution)/shard_map/all_gather | solution.py:85
  86.9 2.9 convolution_convert_fusion.1
  90.8 8.1 %all-to-all-done.4 = bf16[4,256,512]{2,1,0:T(8,128)(2,1)S(1)} async-done(((bf16[4,256,512]{2,1,0:T(8,128)(2,1)}), bf16[4,256,512]{2,1,0:T(8,128)(2,1)S(1)}, u32[]{:S(2)}, u32[]{:S(2)}) %all-to-all-start.4) | async-done | bytes 1048608 | tf_op jit(solution)/shard_map/all_to_all | solution.py:65
  99.0 3.5 %all-to-all-start.1 = ((bf16[4,256,512]{1,2,0:T(8,128)(2,1)}), bf16[4,256,512]{1,2,0:T(8,128)(2,1)S(1)}, u32[]{:S(2)}, u32[]{:S(2)}) async-start(bf16[4,256,512]{1,2,0:T(8,128)(2,1)} %bitcast.109), calls=%async_computation.1 | async-start | bytes 2097152 | tf_op jit(solution)/shard_map/all_to_all | solution.py:76
  102.5 58.3 %all-gather.5.cloned.1.call-done = bf16[1024,1024]{1,0:T(8,128)(2,1)} async-done(((bf16[256,1024]{1,0:T(8,128)(2,1)}), bf16[1024,1024]{1,0:T(8,128)(2,1)}) %all-gather.5.cloned.1.call-update) | async-done | bytes 2097168 | tf_op jit(solution)/shard_map/all_gather | solution.py:86
  160.8 2.9 convolution_convert_fusion
  164.7 3.6 %all-to-all-start.5 = ((bf16[4,256,512]{1,2,0:T(8,128)(2,1)}), bf16[4,256,512]{1,2,0:T(8,128)(2,1)S(1)}, u32[]{:S(2)}, u32[]{:S(2)}) async-start(bf16[4,256,512]{1,2,0:T(8,128)(2,1)} %bitcast.119), calls=%async_computation.5 | async-start | bytes 2097152 | tf_op jit(solution)/shard_map/all_to_all | solution.py:76
  172.1 22.0 %all-to-all-done.5 = bf16[4,256,512]{1,2,0:T(8,128)(2,1)S(1)} async-done(((bf16[4,256,512]{1,2,0:T(8,128)(2,1)}), bf16[4,256,512]{1,2,0:T(8,128)(2,1)S(1)}, u32[]{:S(2)}, u32[]{:S(2)}) %all-to-all-start.5) | async-done | bytes 1048608 | tf_op jit(solution)/shard_map/all_to_all | solution.py:76
  195.6 10.0 %fusion.5 = (bf16[256,4,16,32]{0,3,2,1:T(8,128)(2,1)S(1)}, f32[256,4,16,32]{0,3,2,1:T(8,128)S(1)}) fusion(f32[256,4,16,32]{0,3,2,1:T(8,128)S(1)} %bitcast.112, f32[256]{0:T(256)S(1)} %copy-done.5, f32[256]{0:T(256)S(1)} %bitcast.145, f32[256]{0:T(256)S(1)} %bitcast.147, f32[256]{0:T(256)S(1)} %bitcast.151, f32[256]{0:T(256)S(1)} %bitcast.153, ...), kind=kLoop, calls=%fused_computation.54 | loop fusion | flops 33554432 | bytes 14708736 | tf_op jit(solution)/shard_map/convert_element_type | solution.py:109
  210.7 3.5 %all-to-all-start.2 = ((bf16[4,256,512]{1,2,0:T(8,128)(2,1)}), bf16[4,256,512]{1,2,0:T(8,128)(2,1)S(1)}, u32[]{:S(2)}, u32[]{:S(2)}) async-start(bf16[4,256,512]{1,2,0:T(8,128)(2,1)} %pad_maximum_fusion.1), calls=%async_computation.2 | async-start | bytes 2097152 | tf_op jit(solution)/shard_map/all_to_all | solution.py:65
  215.4 9.3 %fusion.104 = bf16[256,4,16,32]{0,3,2,1:T(8,128)(2,1)S(1)} fusion(f32[256,6,16,32]{0,3,2,1:T(8,128)S(1)} %maximum_convert_fusion.1, f32[256]{0:T(256)S(1)} %bitcast.146, f32[256]{0:T(256)S(1)} %bitcast.148, f32[256]{0:T(256)S(1)} %bitcast.152, f32[256]{0:T(256)S(1)} %bitcast.154, f32[256]{0:T(256)S(1)} %bitcast.156, f32[256]{0:T(256)S(1)} %bitcast.158, ...), kind=kLoop, calls=%fused_computation.153 | loop fusion | flops 28311552 | bytes 10513408 | tf_op jit(solution)/shard_map/convert_element_type | solution.py:113
  226.0 14.3 %all-to-all-done.2 = bf16[4,256,512]{1,2,0:T(8,128)(2,1)S(1)} async-done(((bf16[4,256,512]{1,2,0:T(8,128)(2,1)}), bf16[4,256,512]{1,2,0:T(8,128)(2,1)S(1)}, u32[]{:S(2)}, u32[]{:S(2)}) %all-to-all-start.2) | async-done | bytes 1048608 | tf_op jit(solution)/shard_map/all_to_all | solution.py:65
  240.3 4.4 %all-to-all-start.6 = ((bf16[4,256,512]{1,2,0:T(8,128)(2,1)}), bf16[4,256,512]{1,2,0:T(8,128)(2,1)}, u32[]{:S(2)}, u32[]{:S(2)}) async-start(bf16[4,256,512]{1,2,0:T(8,128)(2,1)} %pad_maximum_fusion.3), calls=%async_computation.6 | async-start | bytes 2097152 | tf_op jit(solution)/shard_map/all_to_all | solution.py:65
  247.4 3.2 fusion.109
  251.9 19.7 %all-to-all-done.6 = bf16[4,256,512]{1,2,0:T(8,128)(2,1)} async-done(((bf16[4,256,512]{1,2,0:T(8,128)(2,1)}), bf16[4,256,512]{1,2,0:T(8,128)(2,1)}, u32[]{:S(2)}, u32[]{:S(2)}) %all-to-all-start.6) | async-done | bytes 1048608 | tf_op jit(solution)/shard_map/all_to_all | solution.py:65
  271.6 3.5 %all-to-all-start.3 = ((bf16[4,256,512]{2,1,0:T(8,128)(2,1)}), bf16[4,256,512]{2,1,0:T(8,128)(2,1)S(1)}, u32[]{:S(2)}, u32[]{:S(2)}) async-start(bf16[4,256,512]{2,1,0:T(8,128)(2,1)} %bitcast.44), calls=%async_computation.3 | async-start | bytes 2097152 | tf_op jit(solution)/shard_map/all_to_all | solution.py:76
  277.2 3.8 %fusion.108 = bf16[1024,512]{0,1:T(8,128)(2,1)} fusion(bf16[1024,512]{0,1:T(8,128)(2,1)S(1)} %copy.48, bf16[1024,512]{1,0:T(8,128)(2,1)S(1)} %bitcast.129, bf16[1024,1024]{1,0:T(8,128)(2,1)} %all-gather.3.cloned.1.call-done), kind=kOutput, calls=%fused_computation.164 | convolution fusion | flops 1075314688 | bytes 5242880 | tf_op jit(solution)/shard_map/dot_general | solution.py:115
  281.0 2.3 copy.49
  283.3 17.9 %all-to-all-done.3 = bf16[4,256,512]{2,1,0:T(8,128)(2,1)S(1)} async-done(((bf16[4,256,512]{2,1,0:T(8,128)(2,1)}), bf16[4,256,512]{2,1,0:T(8,128)(2,1)S(1)}, u32[]{:S(2)}, u32[]{:S(2)}) %all-to-all-start.3) | async-done | bytes 1048608 | tf_op jit(solution)/shard_map/all_to_all | solution.py:76
  301.3 3.5 %all-to-all-start.7 = ((bf16[4,256,512]{2,1,0:T(8,128)(2,1)}), bf16[4,256,512]{2,1,0:T(8,128)(2,1)S(1)}, u32[]{:S(2)}, u32[]{:S(2)}) async-start(bf16[4,256,512]{2,1,0:T(8,128)(2,1)} %bitcast.64), calls=%async_computation.7 | async-start | bytes 2097152 | tf_op jit(solution)/shard_map/all_to_all | solution.py:76
  306.6 23.5 %all-to-all-done.7 = bf16[4,256,512]{2,1,0:T(8,128)(2,1)S(1)} async-done(((bf16[4,256,512]{2,1,0:T(8,128)(2,1)}), bf16[4,256,512]{2,1,0:T(8,128)(2,1)S(1)}, u32[]{:S(2)}, u32[]{:S(2)}) %all-to-all-start.7) | async-done | bytes 1048608 | tf_op jit(solution)/shard_map/all_to_all | solution.py:76
  (52 shorter events, 29.8 us)
Async XLA Ops:
  7.2 79.7 %all-gather.3.cloned.1.call-start = ((), (), s32[]{:S(2)}) async-start(), calls=%async_computation.8 | async-start | bytes 2621440 | tf_op jit(solution)/shard_map/all_gather | solution.py:85
  9.5 8.2 %copy-start.2 = (bf16[256,4,512]{2,1,0:T(4,128)(2,1)S(1)}, bf16[256,4,512]{2,1,0:T(4,128)(2,1)}, u32[]{:S(2)}) copy-start(bf16[256,4,512]{2,1,0:T(4,128)(2,1)} %param.7) | copy-start | bytes 3145732
  10.6 57.5 %all-to-all-start = ((bf16[4,256,512]{2,1,0:T(8,128)(2,1)}), bf16[4,256,512]{2,1,0:T(8,128)(2,1)S(1)}, u32[]{:S(2)}, u32[]{:S(2)}) async-start(bf16[4,256,512]{2,1,0:T(8,128)(2,1)} %pad_maximum_fusion), calls=%async_computation | async-start | bytes 2097152 | tf_op jit(solution)/shard_map/all_to_all | solution.py:65
  17.0 143.8 %all-gather.5.cloned.1.call-start = ((), (), s32[]{:S(2)}) async-start(), calls=%async_computation.9 | async-start | bytes 2621440 | tf_op jit(solution)/shard_map/all_gather | solution.py:86
  68.1 21.7 %copy-start = (bf16[4,256,512]{2,1,0:T(8,128)(2,1)}, bf16[4,256,512]{2,1,0:T(8,128)(2,1)S(1)}, u32[]{:S(2)}) copy-start(bf16[4,256,512]{2,1,0:T(8,128)(2,1)S(1)} %all-to-all-done) | copy-start | bytes 3145732
  68.1 30.9 %all-to-all-start.4 = ((bf16[4,256,512]{2,1,0:T(8,128)(2,1)}), bf16[4,256,512]{2,1,0:T(8,128)(2,1)S(1)}, u32[]{:S(2)}, u32[]{:S(2)}) async-start(bf16[4,256,512]{2,1,0:T(8,128)(2,1)} %pad_maximum_fusion.2), calls=%async_computation.4 | async-start | bytes 2097152 | tf_op jit(solution)/shard_map/all_to_all | solution.py:65
  99.0 65.7 %all-to-all-start.1 = ((bf16[4,256,512]{1,2,0:T(8,128)(2,1)}), bf16[4,256,512]{1,2,0:T(8,128)(2,1)S(1)}, u32[]{:S(2)}, u32[]{:S(2)}) async-start(bf16[4,256,512]{1,2,0:T(8,128)(2,1)} %bitcast.109), calls=%async_computation.1 | async-start | bytes 2097152 | tf_op jit(solution)/shard_map/all_to_all | solution.py:76
  164.7 7.4 %copy-start.4 = (f32[256,27]{0,1:T(8,128)S(1)}, f32[256,27]{0,1:T(8,128)}, u32[]{:S(2)}) copy-start(f32[256,27]{0,1:T(8,128)} %param.10) | copy-start | bytes 82948
  164.7 29.5 %all-to-all-start.5 = ((bf16[4,256,512]{1,2,0:T(8,128)(2,1)}), bf16[4,256,512]{1,2,0:T(8,128)(2,1)S(1)}, u32[]{:S(2)}, u32[]{:S(2)}) async-start(bf16[4,256,512]{1,2,0:T(8,128)(2,1)} %bitcast.119), calls=%async_computation.5 | async-start | bytes 2097152 | tf_op jit(solution)/shard_map/all_to_all | solution.py:76
  169.2 25.2 %collective-permute-start = (bf16[256,1,512]{0,2,1:T(8,128)(2,1)}, bf16[256,1,512]{0,2,1:T(8,128)(2,1)S(1)}, u32[]{:S(2)}, u32[]{:S(2)}) collective-permute-start(bf16[256,1,512]{0,2,1:T(8,128)(2,1)} %get-tuple-element.16), channel_id=1, source_target_pairs={{0,1},{1,2},{2,3},{4,5},{5,6},{6,7},{8,9},{9,10},{10,11},{12,13},{... | collective-permute-start | bytes 786440 | tf_op jit(solution)/shard_map/ppermute | solution.py:17
  170.8 23.6 %collective-permute-start.1 = (bf16[256,1,512]{0,2,1:T(8,128)(2,1)}, bf16[256,1,512]{0,2,1:T(8,128)(2,1)}, u32[]{:S(2)}, u32[]{:S(2)}) collective-permute-start(bf16[256,1,512]{0,2,1:T(8,128)(2,1)} %get-tuple-element.17), channel_id=1, source_target_pairs={{1,0},{2,1},{3,2},{5,4},{6,5},{7,6},{9,8},{10,9},{11,10},{13,12},{... | collective-permute-start | bytes 786440 | tf_op jit(solution)/shard_map/ppermute | solution.py:20
  194.4 1.2 copy-start.5
  206.9 7.3 %collective-permute-start.2 = (bf16[256,1,512]{0,2,1:T(8,128)(2,1)}, bf16[256,1,512]{0,2,1:T(8,128)(2,1)S(1)}, u32[]{:S(2)}, u32[]{:S(2)}) collective-permute-start(bf16[256,1,512]{0,2,1:T(8,128)(2,1)} %get-tuple-element.10), channel_id=1, source_target_pairs={{0,1},{1,2},{2,3},{4,5},{5,6},{6,7},{8,9},{9,10},{10,11},{12,13},{... | collective-permute-start | bytes 786440 | tf_op jit(solution)/shard_map/ppermute | solution.py:17
  208.2 6.0 %collective-permute-start.3 = (bf16[256,1,512]{0,2,1:T(8,128)(2,1)}, bf16[256,1,512]{0,2,1:T(8,128)(2,1)}, u32[]{:S(2)}, u32[]{:S(2)}) collective-permute-start(bf16[256,1,512]{0,2,1:T(8,128)(2,1)} %get-tuple-element.11), channel_id=1, source_target_pairs={{1,0},{2,1},{3,2},{5,4},{6,5},{7,6},{9,8},{10,9},{11,10},{13,12},{... | collective-permute-start | bytes 786440 | tf_op jit(solution)/shard_map/ppermute | solution.py:20
  210.7 29.6 %all-to-all-start.2 = ((bf16[4,256,512]{1,2,0:T(8,128)(2,1)}), bf16[4,256,512]{1,2,0:T(8,128)(2,1)S(1)}, u32[]{:S(2)}, u32[]{:S(2)}) async-start(bf16[4,256,512]{1,2,0:T(8,128)(2,1)} %pad_maximum_fusion.1), calls=%async_computation.2 | async-start | bytes 2097152 | tf_op jit(solution)/shard_map/all_to_all | solution.py:65
  224.8 19.9 %copy-start.1 = (bf16[4,256,512]{2,1,0:T(8,128)(2,1)S(1)}, bf16[4,256,512]{2,1,0:T(8,128)(2,1)}, u32[]{:S(2)}) copy-start(bf16[4,256,512]{2,1,0:T(8,128)(2,1)} %copy-done) | copy-start | bytes 3145732
  240.3 31.3 %all-to-all-start.6 = ((bf16[4,256,512]{1,2,0:T(8,128)(2,1)}), bf16[4,256,512]{1,2,0:T(8,128)(2,1)}, u32[]{:S(2)}, u32[]{:S(2)}) async-start(bf16[4,256,512]{1,2,0:T(8,128)(2,1)} %pad_maximum_fusion.3), calls=%async_computation.6 | async-start | bytes 2097152 | tf_op jit(solution)/shard_map/all_to_all | solution.py:65
  246.1 1.3 copy-start.3
  271.6 29.6 %all-to-all-start.3 = ((bf16[4,256,512]{2,1,0:T(8,128)(2,1)}), bf16[4,256,512]{2,1,0:T(8,128)(2,1)S(1)}, u32[]{:S(2)}, u32[]{:S(2)}) async-start(bf16[4,256,512]{2,1,0:T(8,128)(2,1)} %bitcast.44), calls=%async_computation.3 | async-start | bytes 2097152 | tf_op jit(solution)/shard_map/all_to_all | solution.py:76
  301.3 28.8 %all-to-all-start.7 = ((bf16[4,256,512]{2,1,0:T(8,128)(2,1)}), bf16[4,256,512]{2,1,0:T(8,128)(2,1)S(1)}, u32[]{:S(2)}, u32[]{:S(2)}) async-start(bf16[4,256,512]{2,1,0:T(8,128)(2,1)} %bitcast.64), calls=%async_computation.7 | async-start | bytes 2097152 | tf_op jit(solution)/shard_map/all_to_all | solution.py:76
Sparse Core Ops, SparseCore 0:
  9.5 77.2 all-gather.2
  88.4 72.3 all-gather.4
